TPU v7x, 256 devices: a whole 4x4x8 slice. The times are simulated.
256 devices in a mesh: pole: 8 (over x, y_lo), sub: 32 (over y_hi, z, core).
Axes of the slice: x: 4, y: 4 (y_hi: 2, y_lo: 2; y = y_hi * 2 + y_lo), z: 8, core: 2. Of those that a mesh axis runs over, the one named last changes fastest.
Arguments:
- start_block: float32 [131072, 128], P('sub'), may hold values from -400 to 400
- inverses: float32 [8, 256, 512, 512], P('pole', 'sub'), may hold values from -1 to 3
- iface_rows: int32 [256, 2, 128], P('sub'), may hold values from 0 to 511, as said below
- neighbors: int32 [256, 2], P('sub'), may hold values from 0 to 255, as said below
- couplings: float32 [256, 2, 128], P('sub'), may hold values from 0.25 to 1
- pole_weights: float32 [8], P('pole'), may hold values from 0.25 to 1
Outputs:
- ortho_basis: float32 [131072, 128], P(('sub', 'pole'))
Inputs may be any that keep to these rules, and one draw needn't show every extreme that they name: `iface_rows`: in each subdomain the 256 listed rows are distinct. Subdomain j lies on index j // 8 of sub. neighbors[j, 0] lies on the previous index and neighbors[j, 1] on the next one, cyclically; over the subdomains of one index, the values in column 0 are the previous index's 8 subdomains, each once, and those in column 1 the next index's, each once.
All inputs are finite; a program needn't handle non-finite values.
Results may differ from a plain program's by a relative error of at most 0.0002.
Values sent between devices are 32-bit elements; how exact they have to be, the bound alone decides.
A program may use at most 64 MiB of HBM per device.

v0:
```python
import math

import jax
import jax.numpy as jnp
from jax import lax
from jax.sharding import PartitionSpec as P

precise = lax.Precision.HIGHEST


def extended_2(cells, sides, width):
    for axis, dim in sides:
        count = lax.axis_size(axis)
        head = lax.slice_in_dim(cells, 0, width, axis=dim)
        tail = lax.slice_in_dim(cells, cells.shape[dim] - width, cells.shape[dim], axis=dim)
        cells = jnp.concatenate(
            [
                lax.ppermute(tail, axis, [(i, (i + 1) % count) for i in range(count)]),
                cells,
                lax.ppermute(head, axis, [((i + 1) % count, i) for i in range(count)]),
            ],
            axis=dim,
        )
    return cells


def apply_blocks(blocks, fields):
    return jnp.einsum(
        "sij,sjv->siv", blocks, fields, precision=precise, preferred_element_type=jnp.float32
    )


def add_coupled(fields, iface_rows, neighbor_vals, couplings):

    def one_sub(field_one, rows_one, terms_one):
        field_one = field_one.at[rows_one[0]].add(terms_one[0])
        return field_one.at[rows_one[1]].add(terms_one[1])

    return jax.vmap(one_sub)(fields, iface_rows, couplings[..., None] * neighbor_vals)


def per_device(start_block, inverses, iface_rows, neighbors, couplings, pole_weights):
    blocks = inverses[0]
    sub_count = blocks.shape[0]
    block_len = blocks.shape[1]
    vec_count = start_block.shape[1]
    iface_len = iface_rows.shape[2]
    fields = start_block.reshape(sub_count, block_len, vec_count)
    first_pass = apply_blocks(blocks, fields)
    offsets = (jnp.arange(sub_count, dtype=jnp.int32) * block_len)[:, None, None]
    flat_index = (iface_rows + offsets).transpose(1, 0, 2).reshape(-1)
    outgoing = jnp.take(first_pass.reshape(sub_count * block_len, vec_count), flat_index, axis=0)
    half_rows = sub_count * iface_len
    extended = extended_2(outgoing, (("sub", 0),), half_rows)
    from_prev = extended[:half_rows].reshape(sub_count, iface_len, vec_count)
    from_next = extended[3 * half_rows :].reshape(sub_count, iface_len, vec_count)
    columns = jnp.arange(sub_count, dtype=jnp.int32)[None, :]
    choose_prev = (neighbors[:, 0:1] % sub_count == columns).astype(jnp.float32)
    choose_next = (neighbors[:, 1:2] % sub_count == columns).astype(jnp.float32)
    low_terms = jnp.einsum(
        "jk,kiv->jiv", choose_prev, from_prev, precision=precise, preferred_element_type=jnp.float32
    )
    high_terms = jnp.einsum(
        "jk,kiv->jiv", choose_next, from_next, precision=precise, preferred_element_type=jnp.float32
    )
    corrected = add_coupled(fields, iface_rows, jnp.stack([low_terms, high_terms], 1), couplings)
    weight = pole_weights[0]
    own_rows = sub_count * block_len // lax.axis_size("pole")
    pole_term = weight * apply_blocks(blocks, corrected).reshape(sub_count * block_len, vec_count)
    summed_poles = lax.psum(pole_term, "pole")
    filtered = lax.dynamic_slice_in_dim(
        summed_poles, lax.axis_index("pole") * own_rows, own_rows, 0
    )
    local_gram = jnp.dot(
        filtered.T, filtered, precision=precise, preferred_element_type=jnp.float32
    )
    gram_matrix = lax.psum(local_gram, ("pole", "sub"))
    lower_factor = jnp.linalg.cholesky(gram_matrix)
    total_rows = sub_count * block_len * lax.axis_size("sub")
    solved = lax.linalg.triangular_solve(
        lower_factor, filtered, left_side=False, lower=True, transpose_a=True
    )
    return math.sqrt(total_rows) * solved


def solution(mesh):
    placed = (
        P("sub", None),
        P("pole", "sub", None, None),
        P("sub", None, None),
        P("sub", None),
        P("sub", None, None),
        P("pole"),
    )
    return jax.shard_map(
        per_device, mesh=mesh, in_specs=placed, out_specs=P(("sub", "pole"), None), check_vma=False
    )
```

profile of v0, /device:TPU:1, one launch (start us, length us, event | category | flops | bytes accessed | tf_op | source)
XLA Modules:
  0.0 464.7 jit_solution(7205133361967697777)
XLA Ops:
  6.5 1.6 copy.37
  8.3 10.6 %fusion.2 = f32[8,512,128]{2,1,0:T(8,128)} fusion(f32[8,512,128]{2,1,0:T(8,128)S(1)} %bitcast.62, f32[1,8,512,512]{3,2,1,0:T(8,128)} %param.7), kind=kOutput, calls=%fused_computation.5 | convolution fusion | flops 3221225472 | bytes 12582912 | tf_op jit(solution)/shard_map/sij,sjv->siv/dot_general | solution.py:28
  18.8 7.0 %gather_fusion = f32[2048,128]{1,0:T(8,128)S(1)} fusion(f32[4096,128]{1,0:T(8,128)} %bitcast.64, s32[2048]{0:T(1024)S(1)} %broadcast_clamp_fusion), kind=kCustom, calls=%fused_computation | custom fusion | bytes 2105344 | tf_op jit(solution)/shard_map/jit(_take)/gather | solution.py:52
  25.9 0.3 broadcast_select_fusion
  26.3 1.1 fusion.27
  27.3 3.2 collective-permute-start.1
  31.6 5.8 %collective-permute-done.1 = f32[1024,128]{1,0:T(8,128)S(1)} collective-permute-done((f32[1024,128]{1,0:T(8,128)}, f32[1024,128]{1,0:T(8,128)S(1)}, u32[]{:S(2)}, u32[]{:S(2)}) %collective-permute-start.1) | collective-permute-done | bytes 524320 | tf_op jit(solution)/shard_map/ppermute | solution.py:20
  37.4 0.7 convolution_bitcast_fusion
  38.4 0.7 convolution_bitcast_fusion.1
  39.0 0.3 maximum_multiply_fusion
  39.7 6.8 %scatter_fusion = f32[4096,128]{1,0:T(8,128)S(1)} fusion(f32[4096,128]{1,0:T(8,128)S(1)} %copy.37, s32[1024]{0:T(1024)S(1)} %get-tuple-element.18, f32[1024,128]{1,0:T(8,128)S(1)} %bitcast.67), kind=kCustom, calls=%fused_computation.1 | custom fusion | flops 131072 | bytes 1576960
  46.5 7.0 %scatter_fusion.1 = f32[4096,128]{1,0:T(8,128)S(1)} fusion(f32[4096,128]{1,0:T(8,128)S(1)} %scatter_fusion, s32[1024]{0:T(1024)S(1)} %get-tuple-element.17, f32[1024,128]{1,0:T(8,128)S(1)} %bitcast.66), kind=kCustom, calls=%fused_computation.2 | custom fusion | flops 131072 | bytes 1576960
  53.5 12.6 %multiply_bitcast_fusion = f32[8,512,128]{1,2,0:T(8,128)} fusion(f32[8,512,128]{2,1,0:T(8,128)S(1)} %bitcast.63, f32[1,8,512,512]{3,2,1,0:T(8,128)} %param.7, f32[]{:T(128)} %bitcast.61), kind=kOutput, calls=%fused_computation.7 | convolution fusion | flops 3221749760 | bytes 12582916 | tf_op jit(solution)/shard_map/sij,sjv->siv/dot_general | solution.py:28
  66.1 2.9 copy.20
  69.1 113.2 %all-reduce.3.cloned.1.call-done = f32[4096,128]{1,0:T(8,128)} async-done(((f32[4096,128]{1,0:T(8,128)}), f32[4096,128]{1,0:T(8,128)}) %all-reduce.3.cloned.1.call-update) | async-done | bytes 2097168 | tf_op jit(solution)/shard_map/psum | solution.py:70
  182.3 2.2 fusion.9
  184.6 246.6 %all-reduce.5.cloned.1.call-done = f32[128,128]{0,1:T(8,128)} async-done(((f32[128,128]{0,1:T(8,128)}), f32[128,128]{0,1:T(8,128)}) %all-reduce.5.cloned.1.call-update) | async-done | bytes 65552 | tf_op jit(solution)/shard_map/psum | solution.py:77
  431.2 0.9 copy.22
  432.1 0.9 fusion.13
  433.0 11.7 %cholesky.16 = f32[128,128]{1,0:T(8,128)S(1)} custom-call(f32[128,128]{1,0:T(8,128)S(1)} %fusion.13), custom_call_target="Cholesky" | custom-call | tf_op jit(solution)/shard_map/jit(cholesky)/cholesky | solution.py:78
  444.7 0.6 compare_reduce_fusion
  445.4 0.7 fusion.11
  446.0 9.8 %custom-call.6 = f32[1,128,128]{1,2,0:T(8,128)S(1)} custom-call(f32[1,128,128]{2,1,0:T(8,128)S(1)} %fusion.11), custom_call_target="InvertDiagBlocksLowerTriangular" | custom-call | tf_op jit(solution)/shard_map/triangular_solve | solution.py:80
  455.8 2.0 convolution_multiply_fusion
  (35 shorter events, 1.1 us)
Async XLA Ops:
  6.5 1.6 copy-start
  6.5 175.8 %all-reduce.3.cloned.1.call-start = ((), (), s32[]{:S(2)}) async-start(), calls=%async_computation | async-start | bytes 4194304 | tf_op jit(solution)/shard_map/psum | solution.py:70
  25.9 4.7 %slice-start = ((s32[8,2,128]{2,1,0:T(2,128)}), s32[8,1,128]{2,1,0:T(1,128)S(1)}, s32[]{:S(2)}) async-start(s32[8,2,128]{2,1,0:T(2,128)} %param.8), calls=%async_computation.2 | async-start | bytes 8192 | tf_op jit(solution)/shard_map/vmap()/slice | solution.py:36
  25.9 4.7 %copy-start.2 = (s32[8,2]{0,1:T(2,128)S(1)}, s32[8,2]{0,1:T(2,128)}, u32[]{:S(2)}) copy-start(s32[8,2]{0,1:T(2,128)} %param.9) | copy-start | bytes 196
  25.9 4.7 %copy-start.3 = (s32[2]{0:T(128)S(1)}, s32[2]{0:T(128)}, u32[]{:S(2)}) copy-start(s32[2]{0:T(128)} %constant.95) | copy-start | bytes 28
  25.9 4.8 %copy-start.1 = (f32[8,2,128]{2,1,0:T(2,128)S(1)}, f32[8,2,128]{2,1,0:T(2,128)}, u32[]{:S(2)}) copy-start(f32[8,2,128]{2,1,0:T(2,128)} %param.10) | copy-start | bytes 24580
  25.9 5.6 %copy-start.4 = (s32[2]{0:T(128)S(1)}, s32[2]{0:T(128)}, u32[]{:S(2)}) copy-start(s32[2]{0:T(128)} %constant.98) | copy-start | bytes 28
  27.3 10.1 %collective-permute-start.1 = (f32[1024,128]{1,0:T(8,128)}, f32[1024,128]{1,0:T(8,128)S(1)}, u32[]{:S(2)}, u32[]{:S(2)}) collective-permute-start(f32[1024,128]{1,0:T(8,128)} %get-tuple-element.14), channel_id=1, source_target_pairs={{1,0},{2,1},{3,2},{4,3},{5,4},{6,5},{7,6},{8,7},{9,8},{10,9},{11,1... | collective-permute-start | bytes 1572872 | tf_op jit(solution)/shard_map/ppermute | solution.py:20
  30.5 7.8 %collective-permute-start = (f32[1024,128]{1,0:T(8,128)}, f32[1024,128]{1,0:T(8,128)S(1)}, u32[]{:S(2)}, u32[]{:S(2)}) collective-permute-start(f32[1024,128]{1,0:T(8,128)} %get-tuple-element.13), channel_id=1, source_target_pairs={{0,1},{1,2},{2,3},{3,4},{4,5},{5,6},{6,7},{7,8},{8,9},{9,10},{10,1... | collective-permute-start | bytes 1572872 | tf_op jit(solution)/shard_map/ppermute | solution.py:18
  69.0 362.2 %all-reduce.5.cloned.1.call-start = ((), (), s32[]{:S(2)}) async-start(), calls=%async_computation.1 | async-start | bytes 131072 | tf_op jit(solution)/shard_map/psum | solution.py:77
Sparse Core Ops, SparseCore 0:
  69.2 113.1 all-reduce.2
  187.8 243.3 all-reduce.4
where the time goes:
time: 465 us
  waiting for transfers between devices  366 us (79%)
  other arithmetic  38.4 us (8%)
  matrix products  28.8 us (6%)
  between operations  14.3 us (3%)
  local copies, waits for them, and re-layouts  14 us (3%)
    psum x1, waiting for transfers between devices, per_device(): gram_matrix = lax.psum(local_gram, ('pole', 'sub'))  247 us
    psum x1, waiting for transfers between devices, per_device(): summed_poles = lax.psum(pole_term, 'pole')  113 us
    dot_general x2, matrix products, apply_blocks(): jnp.einsum('sij,sjv->siv', blocks, fields, precision=precise, preferred_e...  23.2 us
    unnamed x5, other arithmetic  13.9 us
    another operation x3, other arithmetic, per_device(): lower_factor = jnp.linalg.cholesky(gram_matrix)  12.4 us
    another operation x2, other arithmetic, per_device(): lax.linalg.triangular_solve(lower_factor, filtered, left_side=False, lowe...  10.5 us
  transfers between devices with their start and end apart: 4, of which 4 were waited for; matrix products, arithmetic and copies ran while one was open for 0% of the time, Pallas kernels for 0%

commit v1 on v0

v1 whole, which is shorter than its diff:
```python
import functools
import math

import jax
import jax.numpy as jnp
from jax import lax
from jax.experimental import pallas as pl
from jax.experimental.pallas import tpu as pltpu
from jax.sharding import PartitionSpec as P

precise = lax.Precision.HIGHEST
MESH = pl.DeviceIdType.MESH
F32 = jnp.float32
BF16 = jnp.bfloat16

SUB = 8
BLK = 512
VEC = 128
IFC = 128
HALF = BLK // 2
NX = 4
NSUB = 32


def pair(value):
    high = value.astype(BF16)
    low = (value - high.astype(F32)).astype(BF16)
    return jnp.concatenate([high, low], axis=1)


def fold(wide):
    return wide[:, :VEC] + wide[:, VEC:]


def mm(a, b):
    return jnp.dot(a, b, preferred_element_type=F32)


def down_lanes(row):
    return jnp.broadcast_to(row, (IFC, IFC)).T


def filter_kernel(
    nb_ref, w_ref, rows_ref, coup_ref, start_ref, inv_ref, out_ref,
    a32, ahl, b32, outgoing, arrived, term, far_l, far_r, near_l, near_r, from_y,
    a_sem, b_sem, ex_send, ex_recv, far_send, far_recv, near_send, near_recv, y_send, y_recv,
):
    pole = lax.axis_index("pole")
    sub = lax.axis_index("sub")
    x = pole // 2
    yl = pole % 2
    other = 1 - yl
    nxt = (sub + 1) % NSUB
    prv = (sub + NSUB - 1) % NSUB
    right = ((x + 1) % NX) * 2 + yl
    left = ((x + NX - 1) % NX) * 2 + yl
    across = x * 2 + other

    def fetch(s):
        return pltpu.make_async_copy(inv_ref.at[s], a32.at[s], a_sem.at[s])

    fetch_b = pltpu.make_async_copy(start_ref, b32, b_sem)
    fetch_b.start()
    for s in range(SUB):
        fetch(s).start()

    barrier = pltpu.get_barrier_semaphore()
    for dev in ((pole, nxt), (pole, prv), (right, sub), (left, sub), (across, sub)):
        pl.semaphore_signal(barrier, inc=1, device_id=dev, device_id_type=MESH)
    pl.semaphore_wait(barrier, 5)
    fetch_b.wait()

    def exchange(side, s):
        return pltpu.make_async_remote_copy(
            src_ref=outgoing.at[side, s],
            dst_ref=arrived.at[1 - side, s],
            send_sem=ex_send.at[side, s],
            recv_sem=ex_recv.at[1 - side, s],
            device_id=(pole, prv if side == 0 else nxt),
            device_id_type=MESH,
        )

    lane_ids = lax.broadcasted_iota(jnp.int32, (IFC, BLK), 1).astype(F32)
    row_ids = lax.broadcasted_iota(jnp.int32, (BLK, 2 * IFC), 0)

    def first(s, carry):
        fetch(s).wait()
        a = a32[s]
        high = a.astype(BF16)
        ahl[s, :, :BLK] = high
        ahl[s, :, BLK:] = (a - high.astype(F32)).astype(BF16)
        b = pair(b32[s])
        first_pass = fold(mm(ahl[s], jnp.concatenate([b, b], axis=0)))
        parts = pair(first_pass)
        rows = rows_ref[s].astype(F32)
        for side in range(2):
            ids = down_lanes(rows[side : side + 1])
            pick = (lane_ids == jnp.concatenate([ids] * (BLK // IFC), axis=1)).astype(F32).astype(BF16)
            outgoing[side, s] = fold(mm(pick, parts))
            exchange(side, s).start()
        return carry

    lax.fori_loop(0, SUB, first, 0)

    def arrive(s, carry):
        exchange(0, s).wait()
        exchange(1, s).wait()
        return carry

    lax.fori_loop(0, SUB, arrive, 0)

    weight = w_ref[0]

    def second(s):
        rows = rows_ref[s]
        coup = coup_ref[s]
        low = arrived[0, lax.rem(nb_ref[s, 0], SUB)] * down_lanes(coup[0:1])
        high = arrived[1, lax.rem(nb_ref[s, 1], SUB)] * down_lanes(coup[1:2])
        terms = pair(jnp.concatenate([low, high], axis=0))
        row = jnp.concatenate([rows[0:1], rows[1:2]], axis=1)
        place = (row_ids == row).astype(F32).astype(BF16)
        corrected = b32[s] + fold(mm(place, terms))
        c = pair(corrected)
        term[s] = weight * fold(mm(ahl[s], jnp.concatenate([c, c], axis=0)))

    lo = pl.ds(0, HALF)
    hi = pl.ds(HALF, HALF)

    def owner(shift, kind):
        return ((x + shift) % NX) * 2 + (other if kind == 0 else yl)

    def send(src, dst, s_sem, r_sem, dev):
        return pltpu.make_async_remote_copy(
            src_ref=src, dst_ref=dst, send_sem=s_sem, recv_sem=r_sem,
            device_id=(dev, sub), device_id_type=MESH,
        )

    def far(kind):
        s = owner(2, kind)
        return (
            send(term.at[s, lo], far_l.at[kind], far_send.at[0, kind], far_recv.at[0, kind], right),
            send(term.at[s, hi], far_r.at[kind], far_send.at[1, kind], far_recv.at[1, kind], left),
        )

    def near(kind, step):
        to_r = hi if step == 0 else lo
        to_l = lo if step == 0 else hi
        return (
            send(term.at[owner(1, kind), to_r], near_l.at[kind, to_r], near_send.at[0, kind, step],
                 near_recv.at[0, kind, step], right),
            send(term.at[owner(3, kind), to_l], near_r.at[kind, to_l], near_send.at[1, kind, step],
                 near_recv.at[1, kind, step], left),
        )

    def sequence(i, carry):
        shift = jnp.where(i < 2, 2, jnp.where(i < 6, 1 + 2 * (i % 2), 0))
        kind = jnp.where(i < 2, i, jnp.where(i < 6, (i - 2) // 2, i - 6))
        s = ((x + shift) % NX) * 2 + jnp.where(kind == 0, other, yl)
        second(s)
        for n in range(2):
            @pl.when(i == n)
            def _():
                for copy in far(n):
                    copy.start()

        @pl.when(i == 2)
        def _():
            near(0, 0)[0].start()

        @pl.when(i == 3)
        def _():
            near(0, 0)[1].start()
        return carry

    lax.fori_loop(0, SUB, sequence, 0)

    def relay(kind):
        far_a, far_b = far(kind)
        s = owner(1, kind)
        far_a.wait_recv()
        term[s, lo] = term[s, lo] + far_l[kind]
        near(kind, 1)[0].start()
        s = owner(3, kind)
        far_b.wait_recv()
        term[s, hi] = term[s, hi] + far_r[kind]
        near(kind, 1)[1].start()

    relay(0)
    for copy in near(1, 0):
        copy.start()
    relay(1)

    def gathered(kind):
        for step in range(2):
            for copy in near(kind, step):
                copy.wait_recv()
        s = owner(0, kind)
        return term[s] + near_l[kind] + near_r[kind]

    term[owner(0, 0)] = gathered(0)
    hand = send(term.at[owner(0, 0)], from_y, y_send, y_recv, across)
    hand.start()
    mine = gathered(1)
    hand.wait_recv()
    out_ref[...] = mine + from_y[...]
    hand.wait_send()
    for kind in range(2):
        for copy in far(kind) + near(kind, 0) + near(kind, 1):
            copy.wait_send()


def filter_call(neighbors, pole_weights, iface_rows, couplings, start, inverses):
    dma = pltpu.SemaphoreType.DMA
    vmem = pl.BlockSpec(memory_space=pltpu.VMEM)
    smem = pl.BlockSpec(memory_space=pltpu.SMEM)
    hbm = pl.BlockSpec(memory_space=pl.ANY)
    return pl.pallas_call(
        filter_kernel,
        name="filter_pass",
        out_shape=jax.ShapeDtypeStruct((BLK, VEC), F32),
        in_specs=[smem, smem, vmem, vmem, hbm, hbm],
        out_specs=vmem,
        scratch_shapes=[
            pltpu.VMEM((SUB, BLK, BLK), F32),
            pltpu.VMEM((SUB, BLK, 2 * BLK), BF16),
            pltpu.VMEM((SUB, BLK, VEC), F32),
            pltpu.VMEM((2, SUB, IFC, VEC), F32),
            pltpu.VMEM((2, SUB, IFC, VEC), F32),
            pltpu.VMEM((SUB, BLK, VEC), F32),
            pltpu.VMEM((2, HALF, VEC), F32),
            pltpu.VMEM((2, HALF, VEC), F32),
            pltpu.VMEM((2, BLK, VEC), F32),
            pltpu.VMEM((2, BLK, VEC), F32),
            pltpu.VMEM((BLK, VEC), F32),
            dma((SUB,)),
            dma,
            dma((2, SUB)),
            dma((2, SUB)),
            dma((2, 2)),
            dma((2, 2)),
            dma((2, 2, 2)),
            dma((2, 2, 2)),
            dma,
            dma,
        ],
        compiler_params=pltpu.CompilerParams(
            collective_id=0, has_side_effects=True, vmem_limit_bytes=56 * 1024 * 1024
        ),
    )(neighbors, pole_weights, iface_rows, couplings, start, inverses)


PIECE = VEC // 8


def gram_kernel(
    f_ref, out_ref,
    local, part, s2, s3, s4, acc2, acc3, full,
    send2, recv2, send3, recv3, send4, recv4, send5, recv5,
):
    pole = lax.axis_index("pole")
    sub = lax.axis_index("sub")
    x = pole // 2
    yl = pole % 2
    yh = sub // 16
    z = (sub // 2) % 8
    core = sub % 2
    y = yh * 2 + yl
    here = x * 2 + core

    def at_xc(d):
        t = (here + d) % 8
        return t, ((t // 2) * 2 + yl, (yh * 8 + z) * 2 + t % 2)

    def at_y(d):
        t = (y + d) % 4
        return (x * 2 + t % 2, ((t // 2) * 8 + z) * 2 + core)

    def at_z(d):
        t = (z + d) % 8
        return (pole, (yh * 8 + t) * 2 + core)

    barrier = pltpu.get_barrier_semaphore()
    for d in range(1, 8):
        pl.semaphore_signal(barrier, inc=1, device_id=at_xc(d)[1], device_id_type=MESH)
        pl.semaphore_signal(barrier, inc=1, device_id=at_z(d), device_id_type=MESH)
    for d in range(1, 4):
        pl.semaphore_signal(barrier, inc=1, device_id=at_y(d), device_id_type=MESH)

    f = f_ref[...]
    local[...] = lax.dot_general(
        f, f, (((0,), (0,)), ((), ())), precision=precise, preferred_element_type=F32
    )
    pl.semaphore_wait(barrier, 17)

    def send(src, dst, s_sem, r_sem, dev):
        return pltpu.make_async_remote_copy(
            src_ref=src, dst_ref=dst, send_sem=s_sem, recv_sem=r_sem,
            device_id=dev, device_id_type=MESH,
        )

    def rows(n):
        return pl.ds(pl.multiple_of(n * PIECE, PIECE), PIECE)

    copies = []
    for d in range(1, 8):
        t, dev = at_xc(d)
        copies.append(send(local.at[rows(t)], s2.at[d - 1], send2.at[d - 1], recv2.at[d - 1], dev))
    for copy in copies:
        copy.start()
    total = local[rows(here)]
    for d in range(7):
        copies[d].wait_recv()
        total = total + s2[d]
    acc2[...] = total

    copies3 = [
        send(acc2, s3.at[d - 1], send3.at[d - 1], recv3.at[d - 1], at_y(d)) for d in range(1, 4)
    ]
    for copy in copies3:
        copy.start()
    for d in range(3):
        copies3[d].wait_recv()
        total = total + s3[d]
    acc3[...] = total

    copies4 = [
        send(acc3, s4.at[d - 1], send4.at[d - 1], recv4.at[d - 1], at_z(d)) for d in range(1, 8)
    ]
    for copy in copies4:
        copy.start()
    for d in range(7):
        copies4[d].wait_recv()
        total = total + s4[d]
    part[...] = total

    copies5 = [
        send(part, full.at[rows(here)], send5.at[d - 1], recv5.at[d - 1], at_xc(d)[1])
        for d in range(1, 8)
    ]
    for copy in copies5:
        copy.start()
    out_ref[rows(here)] = total
    for d in range(1, 8):
        t = (here + 8 - d) % 8
        copies5[d - 1].wait_recv()
        out_ref[rows(t)] = full[rows(t)]
    for copy in copies + copies3 + copies4 + copies5:
        copy.wait_send()


def gram_call(filtered):
    dma = pltpu.SemaphoreType.DMA
    vmem = pl.BlockSpec(memory_space=pltpu.VMEM)
    return pl.pallas_call(
        gram_kernel,
        name="gram_sum",
        out_shape=jax.ShapeDtypeStruct((VEC, VEC), F32),
        in_specs=[vmem],
        out_specs=vmem,
        scratch_shapes=[
            pltpu.VMEM((VEC, VEC), F32),
            pltpu.VMEM((PIECE, VEC), F32),
            pltpu.VMEM((7, PIECE, VEC), F32),
            pltpu.VMEM((3, PIECE, VEC), F32),
            pltpu.VMEM((7, PIECE, VEC), F32),
            pltpu.VMEM((PIECE, VEC), F32),
            pltpu.VMEM((PIECE, VEC), F32),
            pltpu.VMEM((VEC, VEC), F32),
            dma((7,)), dma((7,)), dma((3,)), dma((3,)),
            dma((7,)), dma((7,)), dma((7,)), dma((7,)),
        ],
        compiler_params=pltpu.CompilerParams(collective_id=1, has_side_effects=True),
    )(filtered)


def per_device(start_block, inverses, iface_rows, neighbors, couplings, pole_weights):
    filtered = filter_call(
        neighbors, pole_weights, iface_rows, couplings,
        start_block.reshape(SUB, BLK, VEC), inverses[0],
    )
    gram_matrix = gram_call(filtered)
    lower_factor = jnp.linalg.cholesky(gram_matrix)
    solved = lax.linalg.triangular_solve(
        lower_factor, filtered, left_side=False, lower=True, transpose_a=True
    )
    return math.sqrt(NSUB * SUB * BLK) * solved


def solution(mesh):
    placed = (
        P("sub", None),
        P("pole", "sub", None, None),
        P("sub", None, None),
        P("sub", None),
        P("sub", None, None),
        P("pole"),
    )
    return jax.shard_map(
        per_device, mesh=mesh, in_specs=placed, out_specs=P(("sub", "pole"), None), check_vma=False
    )
```

time: 465 us -> 94.1 us (0.20)
  waiting for transfers between devices: 366 us -> 0 us
  Pallas kernels: 0 us -> 65.1 us
  matrix products: 28.8 us -> 2.02 us
  other arithmetic: 38.4 us -> 23.7 us
  between operations: 14.3 us -> 0.7 us
  local copies, waits for them, and re-layouts: 14 us -> 2.27 us
    psum x2 -> x0, waiting for transfers between devices: 360 us -> none  [the longest x1 247 us: per_device(): gram_matrix = lax.psum(local_gram, ('pole', 'sub'))]
    pallas_call x0 -> x2, Pallas kernels: none -> 65.1 us  [the longest x1 37.4 us: filter_call(): pl.pallas_call(filter_kernel, name='filter_pass', out_shape=jax.ShapeDtyp...]
    dot_general x5 -> x0, matrix products: 26.8 us -> none  [the longest x2 23.2 us: apply_blocks(): jnp.einsum('sij,sjv->siv', blocks, fields, precision=precise, preferred_e...]
    unnamed x5 -> x0, other arithmetic: 13.9 us -> none
    gather x1 -> x0, local copies, waits for them, and re-layouts: 7.05 us -> none  [per_device(): jnp.take(first_pass.reshape(sub_count * block_len, vec_count), flat_index...]
    ppermute x2 -> x0, waiting for transfers between devices: 6.11 us -> none  [the longest x1 5.84 us: extended_2(): lax.ppermute(head, axis, [((i + 1) % count, i) for i in range(count)])]
  transfers between devices with their start and end apart: 4 -> 0, of which waited for: 4 -> 0; matrix products, arithmetic and copies ran while one was open for 0% -> 0% of each run, Pallas kernels for 0% -> 0%
where the time goes in v1:
time: 94.1 us; the launch traced here: 93.8 us
  Pallas kernels  65.1 us (69%)
  other arithmetic  23.7 us (25%)
  local copies, waits for them, and re-layouts  2.27 us (2%)
  matrix products  2.02 us (2%)
    pallas_call x1, Pallas kernels, filter_call(): pl.pallas_call(filter_kernel, name='filter_pass', out_shape=jax.ShapeDtyp...  37.4 us
    pallas_call x1, Pallas kernels, gram_call(): pl.pallas_call(gram_kernel, name='gram_sum', out_shape=jax.ShapeDtypeStru...  27.6 us
    another operation x3, other arithmetic, per_device(): lower_factor = jnp.linalg.cholesky(gram_matrix)  12.4 us
    another operation x2, other arithmetic, per_device(): lax.linalg.triangular_solve(lower_factor, filtered, left_side=False, lowe...  10.5 us
    another operation x1, matrix products, per_device(): lax.linalg.triangular_solve(lower_factor, filtered, left_side=False, lowe...  2.02 us

profile of v1, /device:TPU:1, one launch (start us, length us, event | category | flops | bytes accessed | tf_op | source)
XLA Modules:
  0.0 93.8 jit_solution(2057317100234879447)
XLA Ops:
  0.7 1.3 %copy.7.nb_ref = s32[8,2]{1,0:T(8,128)} copy(s32[8,2]{0,1:T(2,128)} %param.9) | data formatting | bytes 128 | tf_op args[3]
  2.0 37.4 %filter_pass.1.f_ref = f32[512,128]{1,0:T(8,128)} custom-call(s32[8,2]{1,0:T(8,128)} %copy.7.nb_ref, f32[1]{0:T(128)S(6)} %copy.9.w_ref, s32[8,2,128]{2,1,0:T(2,128)} %rows_ref.1, f32[8,2,128]{2,1,0:T(2,128)} %coup_ref.1, f32[8,512,128]{2,1,0:T(8,128)} %bitcast.13, f32[8,512,512]{2,1,0:T(8,128)} %bitcast.12), custom_call_target="tpu_custom_call" | custom-call | tf_op jit(solution)/shard_map/filter_pass/pallas_call | solution.py:217
  39.4 27.6 %gram_sum.1 = f32[128,128]{1,0:T(8,128)} custom-call(f32[512,128]{1,0:T(8,128)} %filter_pass.1.f_ref), custom_call_target="tpu_custom_call" | custom-call | tf_op jit(solution)/shard_map/gram_sum/pallas_call | solution.py:354
  67.1 0.9 copy.8
  68.0 0.9 fusion.2
  68.9 11.7 %cholesky.16 = f32[128,128]{1,0:T(8,128)S(1)} custom-call(f32[128,128]{1,0:T(8,128)S(1)} %fusion.2), custom_call_target="Cholesky" | custom-call | tf_op jit(solution)/shard_map/jit(cholesky)/cholesky | solution.py:382
  80.6 0.6 compare_reduce_fusion
  81.3 0.7 fusion
  81.9 9.8 %custom-call.6 = f32[1,128,128]{1,2,0:T(8,128)S(1)} custom-call(f32[1,128,128]{2,1,0:T(8,128)S(1)} %fusion), custom_call_target="InvertDiagBlocksLowerTriangular" | custom-call | tf_op jit(solution)/shard_map/triangular_solve | solution.py:383
  91.8 2.0 %convolution_multiply_fusion = f32[512,128]{1,0:T(8,128)} fusion(f32[512,128]{1,0:T(8,128)} %filter_pass.1.f_ref, f32[1,128,128]{1,2,0:T(8,128)S(1)} %custom-call.6), kind=kOutput, calls=%fused_computation | convolution fusion | flops 100728832 | bytes 589824 | tf_op jit(solution)/shard_map/triangular_solve | solution.py:383
  (1 shorter events, 0.0 us)

commit v2 on v1

v2 whole, which is shorter than its diff:
```python
import functools
import math

import jax
import jax.numpy as jnp
from jax import lax
from jax.experimental import pallas as pl
from jax.experimental.pallas import tpu as pltpu
from jax.sharding import PartitionSpec as P

precise = lax.Precision.HIGHEST
MESH = pl.DeviceIdType.MESH
F32 = jnp.float32
BF16 = jnp.bfloat16

SUB = 8
BLK = 512
VEC = 128
IFC = 128
HALF = BLK // 2
NX = 4
NSUB = 32


def pair(value):
    high = value.astype(BF16)
    low = (value - high.astype(F32)).astype(BF16)
    return jnp.concatenate([high, low], axis=1)


def fold(wide):
    return wide[:, :VEC] + wide[:, VEC:]


def mm(a, b):
    return jnp.dot(a, b, preferred_element_type=F32)


def down_lanes(row):
    return jnp.broadcast_to(row, (IFC, IFC)).T


def filter_kernel(
    nb_hbm, w_ref, rows_ref, coup_ref, start_ref, inv_ref, out_ref, gram_ref,
    nb_ref, a32, ahl, b32, outgoing, arrived, term, far_l, far_r, near_l, near_r, from_y,
    local, slot2, slot3, slot4, acc2, acc3, part,
    a_sem, b_sem, nb_sem, ex_send, ex_recv, far_send, far_recv, near_send, near_recv,
    y_send, y_recv, send2, recv2, send3, recv3, send4, recv4, send5, recv5,
):
    pole = lax.axis_index("pole")
    sub = lax.axis_index("sub")
    x = pole // 2
    yl = pole % 2
    other = 1 - yl
    yh = sub // 16
    z = (sub // 2) % 8
    core = sub % 2
    y = yh * 2 + yl
    here = x * 2 + core
    nxt = (sub + 1) % NSUB
    prv = (sub + NSUB - 1) % NSUB
    right = ((x + 1) % NX) * 2 + yl
    left = ((x + NX - 1) % NX) * 2 + yl
    across = x * 2 + other

    def at_xc(d):
        t = (here + d) % 8
        return t, ((t // 2) * 2 + yl, (yh * 8 + z) * 2 + t % 2)

    def at_y(d):
        t = (y + d) % 4
        return (x * 2 + t % 2, ((t // 2) * 8 + z) * 2 + core)

    def at_z(d):
        t = (z + d) % 8
        return (pole, (yh * 8 + t) * 2 + core)

    def fetch(s):
        return (
            pltpu.make_async_copy(inv_ref.at[s], a32.at[s], a_sem.at[s]),
            pltpu.make_async_copy(start_ref.at[s], b32.at[s], b_sem.at[s]),
        )

    fetch_nb = pltpu.make_async_copy(nb_hbm, nb_ref, nb_sem)
    for s in range(SUB):
        for copy in fetch(s):
            copy.start()
    fetch_nb.start()

    barrier = pltpu.get_barrier_semaphore()
    peers = [(pole, nxt), (pole, prv)]
    peers += [at_xc(d)[1] for d in range(1, 8)]
    peers += [at_y(d) for d in range(1, 4)]
    peers += [at_z(d) for d in range(1, 8)]
    for dev in peers:
        pl.semaphore_signal(barrier, inc=1, device_id=dev, device_id_type=MESH)

    def send(src, dst, s_sem, r_sem, dev):
        return pltpu.make_async_remote_copy(
            src_ref=src, dst_ref=dst, send_sem=s_sem, recv_sem=r_sem,
            device_id=dev, device_id_type=MESH,
        )

    def exchange(side, s):
        return send(
            outgoing.at[side, s], arrived.at[1 - side, s],
            ex_send.at[side, s], ex_recv.at[1 - side, s],
            (pole, prv if side == 0 else nxt),
        )

    lane_ids = lax.broadcasted_iota(jnp.int32, (IFC, BLK), 1).astype(F32)
    row_ids = lax.broadcasted_iota(jnp.int32, (BLK, 2 * IFC), 0)

    def apply(s, vectors):
        parts = pair(vectors)
        return fold(mm(ahl[s, :, :BLK], parts)) + mm(ahl[s, :, BLK:], parts[:, :VEC])

    def first(s, carry):
        for copy in fetch(s):
            copy.wait()
        a = a32[s]
        high = a.astype(BF16)
        ahl[s, :, :BLK] = high
        ahl[s, :, BLK:] = (a - high.astype(F32)).astype(BF16)
        parts = pair(apply(s, b32[s]))
        rows = rows_ref[s].astype(F32)
        for side in range(2):
            ids = down_lanes(rows[side : side + 1])
            pick = (lane_ids == jnp.concatenate([ids] * (BLK // IFC), axis=1)).astype(F32).astype(BF16)
            outgoing[side, s] = fold(mm(pick, parts))

        @pl.when(s == 0)
        def _():
            pl.semaphore_wait(barrier, len(peers))

        for side in range(2):
            exchange(side, s).start()
        return carry

    lax.fori_loop(0, SUB, first, 0)
    fetch_nb.wait()

    def arrive(s, carry):
        exchange(0, s).wait()
        exchange(1, s).wait()
        return carry

    lax.fori_loop(0, SUB, arrive, 0)

    weight = w_ref[0]

    def second(s):
        rows = rows_ref[s]
        coup = coup_ref[s]
        low = arrived[0, lax.rem(nb_ref[0, s], SUB)] * down_lanes(coup[0:1])
        high = arrived[1, lax.rem(nb_ref[1, s], SUB)] * down_lanes(coup[1:2])
        terms = pair(jnp.concatenate([low, high], axis=0))
        row = jnp.concatenate([rows[0:1], rows[1:2]], axis=1)
        place = (row_ids == row).astype(F32).astype(BF16)
        term[s] = weight * apply(s, b32[s] + fold(mm(place, terms)))

    lo = pl.ds(0, HALF)
    hi = pl.ds(HALF, HALF)

    def owner(shift, kind):
        return ((x + shift) % NX) * 2 + (other if kind == 0 else yl)

    def far(kind):
        s = owner(2, kind)
        return (
            send(term.at[s, lo], far_l.at[kind], far_send.at[0, kind], far_recv.at[0, kind], (right, sub)),
            send(term.at[s, hi], far_r.at[kind], far_send.at[1, kind], far_recv.at[1, kind], (left, sub)),
        )

    def near(kind, step):
        to_r = hi if step == 0 else lo
        to_l = lo if step == 0 else hi
        return (
            send(term.at[owner(1, kind), to_r], near_l.at[kind, to_r], near_send.at[0, kind, step],
                 near_recv.at[0, kind, step], (right, sub)),
            send(term.at[owner(3, kind), to_l], near_r.at[kind, to_l], near_send.at[1, kind, step],
                 near_recv.at[1, kind, step], (left, sub)),
        )

    def sequence(i, carry):
        shift = jnp.where(i < 2, 2, jnp.where(i < 6, 1 + 2 * (i % 2), 0))
        kind = jnp.where(i < 2, i, jnp.where(i < 6, (i - 2) // 2, i - 6))
        second(((x + shift) % NX) * 2 + jnp.where(kind == 0, other, yl))
        for n in range(2):
            @pl.when(i == n)
            def _():
                for copy in far(n):
                    copy.start()

        @pl.when(i == 2)
        def _():
            near(0, 0)[0].start()

        @pl.when(i == 3)
        def _():
            near(0, 0)[1].start()
        return carry

    lax.fori_loop(0, SUB, sequence, 0)

    def relay(kind):
        far_a, far_b = far(kind)
        s = owner(1, kind)
        far_a.wait_recv()
        term[s, lo] = term[s, lo] + far_l[kind]
        near(kind, 1)[0].start()
        s = owner(3, kind)
        far_b.wait_recv()
        term[s, hi] = term[s, hi] + far_r[kind]
        near(kind, 1)[1].start()

    relay(0)
    for copy in near(1, 0):
        copy.start()
    relay(1)

    def gathered(kind):
        for step in range(2):
            for copy in near(kind, step):
                copy.wait_recv()
        return term[owner(0, kind)] + near_l[kind] + near_r[kind]

    term[owner(0, 0)] = gathered(0)
    hand = send(term.at[owner(0, 0)], from_y, y_send, y_recv, (across, sub))
    hand.start()
    mine = gathered(1)
    hand.wait_recv()
    mine = mine + from_y[...]
    out_ref[...] = mine

    parts = pair(mine)
    four = lax.dot_general(parts, parts, (((0,), (0,)), ((), ())), preferred_element_type=F32)
    local[...] = fold(four[:VEC]) + fold(four[VEC:])

    def rows_of(n):
        return pl.ds(pl.multiple_of(n * PIECE, PIECE), PIECE)

    copies2 = []
    for d in range(1, 8):
        t, dev = at_xc(d)
        copies2.append(send(local.at[rows_of(t)], slot2.at[d - 1], send2.at[d - 1], recv2.at[d - 1], dev))
    for copy in copies2:
        copy.start()
    total = local[rows_of(here)]
    for d in range(7):
        copies2[d].wait_recv()
        total = total + slot2[d]
    acc2[...] = total

    copies3 = [
        send(acc2, slot3.at[d - 1], send3.at[d - 1], recv3.at[d - 1], at_y(d)) for d in range(1, 4)
    ]
    for copy in copies3:
        copy.start()
    for d in range(3):
        copies3[d].wait_recv()
        total = total + slot3[d]
    acc3[...] = total

    copies4 = [
        send(acc3, slot4.at[d - 1], send4.at[d - 1], recv4.at[d - 1], at_z(d)) for d in range(1, 8)
    ]
    for copy in copies4:
        copy.start()
    for d in range(7):
        copies4[d].wait_recv()
        total = total + slot4[d]
    part[...] = total
    gram_ref[rows_of(here)] = total

    copies5 = [
        send(part, gram_ref.at[rows_of(here)], send5.at[d - 1], recv5.at[d - 1], at_xc(d)[1])
        for d in range(1, 8)
    ]
    for copy in copies5:
        copy.start()
    hand.wait_send()
    for kind in range(2):
        for copy in far(kind) + near(kind, 0) + near(kind, 1):
            copy.wait_send()
    for copy in copies2 + copies3 + copies4:
        copy.wait_send()
    for copy in copies5:
        copy.wait()


PIECE = VEC // 8


def filter_call(neighbors, pole_weights, iface_rows, couplings, start, inverses):
    dma = pltpu.SemaphoreType.DMA
    vmem = pl.BlockSpec(memory_space=pltpu.VMEM)
    smem = pl.BlockSpec(memory_space=pltpu.SMEM)
    hbm = pl.BlockSpec(memory_space=pl.ANY)
    return pl.pallas_call(
        filter_kernel,
        name="filter_pass",
        out_shape=(
            jax.ShapeDtypeStruct((BLK, VEC), F32),
            jax.ShapeDtypeStruct((VEC, VEC), F32),
        ),
        in_specs=[hbm, smem, vmem, vmem, hbm, hbm],
        out_specs=(vmem, vmem),
        scratch_shapes=[
            pltpu.SMEM((2, SUB), jnp.int32),
            pltpu.VMEM((SUB, BLK, BLK), F32),
            pltpu.VMEM((SUB, BLK, 2 * BLK), BF16),
            pltpu.VMEM((SUB, BLK, VEC), F32),
            pltpu.VMEM((2, SUB, IFC, VEC), F32),
            pltpu.VMEM((2, SUB, IFC, VEC), F32),
            pltpu.VMEM((SUB, BLK, VEC), F32),
            pltpu.VMEM((2, HALF, VEC), F32),
            pltpu.VMEM((2, HALF, VEC), F32),
            pltpu.VMEM((2, BLK, VEC), F32),
            pltpu.VMEM((2, BLK, VEC), F32),
            pltpu.VMEM((BLK, VEC), F32),
            pltpu.VMEM((VEC, VEC), F32),
            pltpu.VMEM((7, PIECE, VEC), F32),
            pltpu.VMEM((3, PIECE, VEC), F32),
            pltpu.VMEM((7, PIECE, VEC), F32),
            pltpu.VMEM((PIECE, VEC), F32),
            pltpu.VMEM((PIECE, VEC), F32),
            pltpu.VMEM((PIECE, VEC), F32),
            dma((SUB,)), dma((SUB,)), dma,
            dma((2, SUB)), dma((2, SUB)),
            dma((2, 2)), dma((2, 2)),
            dma((2, 2, 2)), dma((2, 2, 2)),
            dma, dma,
            dma((7,)), dma((7,)), dma((3,)), dma((3,)),
            dma((7,)), dma((7,)), dma((7,)), dma((7,)),
        ],
        compiler_params=pltpu.CompilerParams(
            collective_id=0, has_side_effects=True, vmem_limit_bytes=56 * 1024 * 1024
        ),
    )(neighbors, pole_weights, iface_rows, couplings, start, inverses)


TILE = 8


def spread(row):
    return jnp.broadcast_to(row, (TILE, VEC))


def ortho_kernel(scale, g_ref, f_ref, out_ref, w_ref):
    count = VEC // TILE
    tiles = [g_ref[TILE * t : TILE * t + TILE, :] for t in range(count)]
    sub = lax.broadcasted_iota(jnp.int32, (TILE, VEC), 0)
    lane = lax.broadcasted_iota(jnp.int32, (TILE, VEC), 1)
    for p in range(count):
        c0 = TILE * p
        cols = {
            (m, t): jnp.broadcast_to(tiles[t][:, c0 + m : c0 + m + 1], (TILE, VEC))
            for t in range(p, count)
            for m in range(TILE)
        }
        panel = (lane >= c0) & (lane < c0 + TILE)
        pivots = jnp.ones((TILE, VEC), F32)
        top = jnp.where(panel, (lane - c0 == sub).astype(F32), tiles[p])
        factors = {}
        for k in range(TILE):
            pivot = spread(cols[k, p][k : k + 1])
            pivots = jnp.where(sub == k, pivot, pivots)
            inverse = 1.0 / pivot
            upper = {m: spread(cols[m, p][k : k + 1]) for m in range(k + 1, TILE)}
            f = jnp.where(sub > k, cols[k, p] * inverse, 0.0)
            for m in range(k + 1, TILE):
                cols[m, p] = cols[m, p] - f * upper[m]
            top = top - f * spread(top[k : k + 1])
            for t in range(p + 1, count):
                f = cols[k, t] * inverse
                factors[k, t] = f
                for m in range(k + 1, TILE):
                    cols[m, t] = cols[m, t] - f * upper[m]
        rows = [spread(top[k : k + 1]) for k in range(TILE)]
        for t in range(p + 1, count):
            value = jnp.where(panel, 0.0, tiles[t])
            for k in range(TILE):
                value = value - factors[k, t] * rows[k]
            tiles[t] = value
        w_ref[c0 : c0 + TILE, :] = jnp.where(lane <= sub + c0, top * (scale * lax.rsqrt(pivots)), 0.0)
    out_ref[...] = lax.dot_general(
        f_ref[...], w_ref[...], (((1,), (1,)), ((), ())), precision=precise, preferred_element_type=F32
    )


def ortho_call(gram_matrix, filtered, scale):
    vmem = pl.BlockSpec(memory_space=pltpu.VMEM)
    return pl.pallas_call(
        functools.partial(ortho_kernel, scale),
        name="ortho",
        out_shape=jax.ShapeDtypeStruct((BLK, VEC), F32),
        in_specs=[vmem, vmem],
        out_specs=vmem,
        scratch_shapes=[pltpu.VMEM((VEC, VEC), F32)],
    )(gram_matrix, filtered)


def per_device(start_block, inverses, iface_rows, neighbors, couplings, pole_weights):
    filtered, gram_matrix = filter_call(
        neighbors.T, pole_weights, iface_rows, couplings,
        start_block.reshape(SUB, BLK, VEC), inverses[0],
    )
    return ortho_call(gram_matrix, filtered, math.sqrt(NSUB * SUB * BLK))


def solution(mesh):
    placed = (
        P("sub", None),
        P("pole", "sub", None, None),
        P("sub", None, None),
        P("sub", None),
        P("sub", None, None),
        P("pole"),
    )
    return jax.shard_map(
        per_device, mesh=mesh, in_specs=placed, out_specs=P(("sub", "pole"), None), check_vma=False
    )
```

time: 94.1 us -> 65.3 us (0.69)
  other arithmetic: 23.7 us -> 0 us
  local copies, waits for them, and re-layouts: 2.27 us -> 0 us
  matrix products: 2.02 us -> 0 us
    another operation x5 -> x0, other arithmetic: 22.9 us -> none  [the longest x3 12.4 us: per_device(): lower_factor = jnp.linalg.cholesky(gram_matrix)]
    another operation x1 -> x0, matrix products: 2.02 us -> none  [per_device(): lax.linalg.triangular_solve(lower_factor, filtered, left_side=False, lowe...]
    unnamed x1 -> x0, local copies, waits for them, and re-layouts: 1.35 us -> none
where the time goes in v2:
time: 65.3 us; the launch traced here: 65.1 us
  Pallas kernels  64.5 us (99%)
  between operations  0.66 us (1%)
    pallas_call x1, Pallas kernels, filter_call(): pl.pallas_call(filter_kernel, name='filter_pass', out_shape=(jax.ShapeDty...  58.2 us
    pallas_call x1, Pallas kernels, ortho_call(): pl.pallas_call(functools.partial(ortho_kernel, scale), name='ortho', out_...  6.23 us

profile of v2, /device:TPU:1, one launch (start us, length us, event | category | flops | bytes accessed | tf_op | source)
XLA Modules:
  0.0 65.1 jit_solution(16062437353533405371)
XLA Ops:
  0.7 58.2 %filter_pass.1 = (f32[512,128]{1,0:T(8,128)}, f32[128,128]{1,0:T(8,128)}) custom-call(s32[2,8]{1,0:T(2,128)} %bitcast.5, f32[1]{0:T(128)S(6)} %copy.7.w_ref, s32[8,2,128]{2,1,0:T(2,128)} %rows_ref.1, f32[8,2,128]{2,1,0:T(2,128)} %coup_ref.1, f32[8,512,128]{2,1,0:T(8,128)} %bitcast.4, f32[8,512,512]{2,1,0:T(8,128)} %bitcast.3), custom_call_target="tpu_custom_call" | custom-call | tf_op jit(solution)/shard_map/filter_pass/pallas_call | solution.py:300
  58.9 6.2 %ortho.1 = f32[512,128]{1,0:T(8,128)} custom-call(f32[128,128]{1,0:T(8,128)} %get-tuple-element.7.g_ref, f32[512,128]{1,0:T(8,128)} %get-tuple-element.8.f_ref), custom_call_target="tpu_custom_call" | custom-call | tf_op jit(solution)/shard_map/ortho/pallas_call | solution.py:394

commit v3 on v2

--- a/solution.py
+++ b/solution.py
@@ -17,7 +17,8 @@
 BLK = 512
 VEC = 128
 IFC = 128
-HALF = BLK // 2
+XROWS = 288
+YROWS = BLK - XROWS
 NX = 4
 NSUB = 32
 
@@ -42,10 +43,10 @@
 
 def filter_kernel(
     nb_hbm, w_ref, rows_ref, coup_ref, start_ref, inv_ref, out_ref, gram_ref,
-    nb_ref, a32, ahl, b32, outgoing, arrived, term, far_l, far_r, near_l, near_r, from_y,
+    nb_ref, a32, ahl, b32, outgoing, arrived, term, far_l, far_r, far_l2, far_r2, near_l, near_r, crossed, from_y,
     local, slot2, slot3, slot4, acc2, acc3, part,
     a_sem, b_sem, nb_sem, ex_send, ex_recv, far_send, far_recv, near_send, near_recv,
-    y_send, y_recv, send2, recv2, send3, recv3, send4, recv4, send5, recv5,
+    cross_send, cross_recv, y_send, y_recv, send2, recv2, send3, recv3, send4, recv4, send5, recv5,
 ):
     pole = lax.axis_index("pole")
     sub = lax.axis_index("sub")
@@ -159,78 +160,119 @@
         place = (row_ids == row).astype(F32).astype(BF16)
         term[s] = weight * apply(s, b32[s] + fold(mm(place, terms)))
 
-    lo = pl.ds(0, HALF)
-    hi = pl.ds(HALF, HALF)
-
     def owner(shift, kind):
         return ((x + shift) % NX) * 2 + (other if kind == 0 else yl)
 
+    lo, hi = pl.ds(0, XROWS // 2), pl.ds(XROWS // 2, XROWS // 2)
+    ylo, yhi = pl.ds(XROWS, YROWS // 2), pl.ds(XROWS + YROWS // 2, YROWS // 2)
+    xrows, yrows = pl.ds(0, XROWS), pl.ds(XROWS, YROWS)
+
     def far(kind):
-        s = owner(2, kind)
+        s = owner(2, min(kind, 1))
+        to_r, to_l = (lo, hi) if kind < 2 else (ylo, yhi)
+        dst_r = far_l.at[kind] if kind < 2 else far_l2
+        dst_l = far_r.at[kind] if kind < 2 else far_r2
         return (
-            send(term.at[s, lo], far_l.at[kind], far_send.at[0, kind], far_recv.at[0, kind], (right, sub)),
-            send(term.at[s, hi], far_r.at[kind], far_send.at[1, kind], far_recv.at[1, kind], (left, sub)),
+            send(term.at[s, to_r], dst_r, far_send.at[0, kind], far_recv.at[0, kind], (right, sub)),
+            send(term.at[s, to_l], dst_l, far_send.at[1, kind], far_recv.at[1, kind], (left, sub)),
         )
 
     def near(kind, step):
-        to_r = hi if step == 0 else lo
-        to_l = lo if step == 0 else hi
+        low, high = (lo, hi) if kind < 2 else (ylo, yhi)
+        to_r, to_l = (high, low) if step == 0 else (low, high)
+        s, slot = min(kind, 1), min(kind, 1)
         return (
-            send(term.at[owner(1, kind), to_r], near_l.at[kind, to_r], near_send.at[0, kind, step],
+            send(term.at[owner(1, s), to_r], near_l.at[slot, to_r], near_send.at[0, kind, step],
                  near_recv.at[0, kind, step], (right, sub)),
-            send(term.at[owner(3, kind), to_l], near_r.at[kind, to_l], near_send.at[1, kind, step],
+            send(term.at[owner(3, s), to_l], near_r.at[slot, to_l], near_send.at[1, kind, step],
                  near_recv.at[1, kind, step], (left, sub)),
         )
 
-    def sequence(i, carry):
-        shift = jnp.where(i < 2, 2, jnp.where(i < 6, 1 + 2 * (i % 2), 0))
-        kind = jnp.where(i < 2, i, jnp.where(i < 6, (i - 2) // 2, i - 6))
-        second(((x + shift) % NX) * 2 + jnp.where(kind == 0, other, yl))
-        for n in range(2):
-            @pl.when(i == n)
-            def _():
-                for copy in far(n):
-                    copy.start()
-
-        @pl.when(i == 2)
-        def _():
-            near(0, 0)[0].start()
-
-        @pl.when(i == 3)
-        def _():
-            near(0, 0)[1].start()
-        return carry
-
-    lax.fori_loop(0, SUB, sequence, 0)
+    def cross(shift):
+        return send(
+            term.at[owner(shift, 0), yrows], crossed.at[shift],
+            cross_send.at[shift], cross_recv.at[shift], (across, sub),
+        )
 
     def relay(kind):
         far_a, far_b = far(kind)
-        s = owner(1, kind)
+        low, high = (lo, hi) if kind < 2 else (ylo, yhi)
+        s = owner(1, min(kind, 1))
         far_a.wait_recv()
-        term[s, lo] = term[s, lo] + far_l[kind]
+        term[s, low] = term[s, low] + (far_l[kind] if kind < 2 else far_l2[...])
         near(kind, 1)[0].start()
-        s = owner(3, kind)
+        s = owner(3, min(kind, 1))
         far_b.wait_recv()
-        term[s, hi] = term[s, hi] + far_r[kind]
+        term[s, high] = term[s, high] + (far_r[kind] if kind < 2 else far_r2[...])
         near(kind, 1)[1].start()
 
-    relay(0)
-    for copy in near(1, 0):
+    def join(shift):
+        cross(shift).wait_recv()
+        s = owner(shift, 1)
+        term[s, yrows] = term[s, yrows] + crossed[shift]
+
+    def sequence(i, carry):
+        shift = jnp.where(i < 2, 2, jnp.where(i < 5, (2 * i - 3) % 4, (2 * i - 9) % 4))
+        shift = jnp.where((i == 4) | (i == 7), 0, shift)
+        kind = jnp.where((i == 1) | (i > 4), 1, 0)
+
+        @pl.when(i == 7)
+        def _():
+            relay(0)
+
+        second(((x + shift) % NX) * 2 + jnp.where(kind == 0, other, yl))
+
+        @pl.when(i == 0)
+        def _():
+            far(0)[0].start()
+            far(0)[1].start()
+            cross(2).start()
+
+        @pl.when(i == 1)
+        def _():
+            far(1)[0].start()
+            far(1)[1].start()
+
+        @pl.when(i == 2)
+        def _():
+            near(0, 0)[0].start()
+            cross(1).start()
+
+        @pl.when(i == 3)
+        def _():
+            near(0, 0)[1].start()
+            cross(3).start()
+
+        @pl.when(i == 4)
+        def _():
+            cross(0).start()
+        return carry
+
+    lax.fori_loop(0, SUB, sequence, 0)
+
+    join(2)
+    for copy in far(2) + near(1, 0):
         copy.start()
     relay(1)
-
-    def gathered(kind):
-        for step in range(2):
-            for copy in near(kind, step):
-                copy.wait_recv()
-        return term[owner(0, kind)] + near_l[kind] + near_r[kind]
-
-    term[owner(0, 0)] = gathered(0)
-    hand = send(term.at[owner(0, 0)], from_y, y_send, y_recv, (across, sub))
+    join(1)
+    near(2, 0)[0].start()
+    join(3)
+    near(2, 0)[1].start()
+
+    own = owner(0, 0)
+    for copy in near(0, 0) + near(0, 1):
+        copy.wait_recv()
+    term[own, xrows] = term[own, xrows] + near_l[0, xrows] + near_r[0, xrows]
+    hand = send(term.at[own, xrows], from_y, y_send, y_recv, (across, sub))
     hand.start()
-    mine = gathered(1)
+    relay(2)
+    join(0)
+    for copy in near(1, 0) + near(1, 1) + near(2, 0) + near(2, 1):
+        copy.wait_recv()
+    own = owner(0, 1)
     hand.wait_recv()
-    mine = mine + from_y[...]
+    term[own, xrows] = term[own, xrows] + from_y[...]
+    mine = term[own] + near_l[1] + near_r[1]
     out_ref[...] = mine
 
     parts = pair(mine)
@@ -280,9 +322,11 @@
     for copy in copies5:
         copy.start()
     hand.wait_send()
-    for kind in range(2):
+    for kind in range(3):
         for copy in far(kind) + near(kind, 0) + near(kind, 1):
             copy.wait_send()
+    for shift in range(NX):
+        cross(shift).wait_send()
     for copy in copies2 + copies3 + copies4:
         copy.wait_send()
     for copy in copies5:
@@ -314,11 +358,14 @@
             pltpu.VMEM((2, SUB, IFC, VEC), F32),
             pltpu.VMEM((2, SUB, IFC, VEC), F32),
             pltpu.VMEM((SUB, BLK, VEC), F32),
-            pltpu.VMEM((2, HALF, VEC), F32),
-            pltpu.VMEM((2, HALF, VEC), F32),
+            pltpu.VMEM((2, XROWS // 2, VEC), F32),
+            pltpu.VMEM((2, XROWS // 2, VEC), F32),
+            pltpu.VMEM((YROWS // 2, VEC), F32),
+            pltpu.VMEM((YROWS // 2, VEC), F32),
             pltpu.VMEM((2, BLK, VEC), F32),
             pltpu.VMEM((2, BLK, VEC), F32),
-            pltpu.VMEM((BLK, VEC), F32),
+            pltpu.VMEM((NX, YROWS, VEC), F32),
+            pltpu.VMEM((XROWS, VEC), F32),
             pltpu.VMEM((VEC, VEC), F32),
             pltpu.VMEM((7, PIECE, VEC), F32),
             pltpu.VMEM((3, PIECE, VEC), F32),
@@ -328,9 +375,9 @@
             pltpu.VMEM((PIECE, VEC), F32),
             dma((SUB,)), dma((SUB,)), dma,
             dma((2, SUB)), dma((2, SUB)),
-            dma((2, 2)), dma((2, 2)),
-            dma((2, 2, 2)), dma((2, 2, 2)),
-            dma, dma,
+            dma((2, 3)), dma((2, 3)),
+            dma((2, 3, 2)), dma((2, 3, 2)),
+            dma((NX,)), dma((NX,)), dma, dma,
             dma((7,)), dma((7,)), dma((3,)), dma((3,)),
             dma((7,)), dma((7,)), dma((7,)), dma((7,)),
         ],

time: 65.3 us -> 60.6 us (0.928)
  Pallas kernels: 64.5 us -> 59.7 us
    pallas_call x1, Pallas kernels: 58.2 us -> 53.5 us  [filter_call(): pl.pallas_call(filter_kernel, name='filter_pass', out_shape=(jax.ShapeDty...]
where the time goes in v3:
time: 60.6 us; the launch traced here: 60.4 us
  Pallas kernels  59.7 us (99%)
  between operations  0.66 us (1%)
    pallas_call x1, Pallas kernels, filter_call(): pl.pallas_call(filter_kernel, name='filter_pass', out_shape=(jax.ShapeDty...  53.5 us
    pallas_call x1, Pallas kernels, ortho_call(): pl.pallas_call(functools.partial(ortho_kernel, scale), name='ortho', out_...  6.23 us

profile of v3, /device:TPU:1, one launch (start us, length us, event | category | flops | bytes accessed | tf_op | source)
XLA Modules:
  0.0 60.4 jit_solution(8034297577190630623)
XLA Ops:
  0.7 53.5 %filter_pass.1 = (f32[512,128]{1,0:T(8,128)}, f32[128,128]{1,0:T(8,128)}) custom-call(s32[2,8]{1,0:T(2,128)} %bitcast.5, f32[1]{0:T(128)S(6)} %copy.7.w_ref, s32[8,2,128]{2,1,0:T(2,128)} %rows_ref.1, f32[8,2,128]{2,1,0:T(2,128)} %coup_ref.1, f32[8,512,128]{2,1,0:T(8,128)} %bitcast.4, f32[8,512,512]{2,1,0:T(8,128)} %bitcast.3), custom_call_target="tpu_custom_call" | custom-call | tf_op jit(solution)/shard_map/filter_pass/pallas_call | solution.py:344
  54.1 6.2 %ortho.1 = f32[512,128]{1,0:T(8,128)} custom-call(f32[128,128]{1,0:T(8,128)} %get-tuple-element.7.g_ref, f32[512,128]{1,0:T(8,128)} %get-tuple-element.8.f_ref), custom_call_target="tpu_custom_call" | custom-call | tf_op jit(solution)/shard_map/ortho/pallas_call | solution.py:441

commit v4 on v3

--- a/solution.py
+++ b/solution.py
@@ -17,6 +17,9 @@
 BLK = 512
 VEC = 128
 IFC = 128
+PIECE = VEC // 8
+EIGHT = (4, 3, 5, 2, 6, 1, 7)
+FOUR = (2, 1, 3)
 XROWS = 288
 YROWS = BLK - XROWS
 NX = 4
@@ -43,9 +46,9 @@
 
 def filter_kernel(
     nb_hbm, w_ref, rows_ref, coup_ref, start_ref, inv_ref, out_ref, gram_ref,
-    nb_ref, a32, ahl, b32, outgoing, arrived, term, far_l, far_r, far_l2, far_r2, near_l, near_r, crossed, from_y,
+    nb_ref, a32, ahl, b32, outgoing, arrived, term, far_l, far_r, far_l2, far_r2, near_l, near_r, crossed, from_y, held,
     local, slot2, slot3, slot4, acc2, acc3, part,
-    a_sem, b_sem, nb_sem, ex_send, ex_recv, far_send, far_recv, near_send, near_recv,
+    a_sem, b_sem, nb_sem, out_sem, ex_send, ex_recv, far_send, far_recv, near_send, near_recv,
     cross_send, cross_recv, y_send, y_recv, send2, recv2, send3, recv3, send4, recv4, send5, recv5,
 ):
     pole = lax.axis_index("pole")
@@ -83,18 +86,19 @@
         )
 
     fetch_nb = pltpu.make_async_copy(nb_hbm, nb_ref, nb_sem)
-    for s in range(SUB):
+    for copy in fetch(0):
+        copy.start()
+    barrier = pltpu.get_barrier_semaphore()
+    peers = [at_z(d) for d in EIGHT]
+    peers += [(pole, nxt), (pole, prv)]
+    peers += [at_y(d) for d in FOUR]
+    peers += [at_xc(d)[1] for d in EIGHT]
+    for dev in peers:
+        pl.semaphore_signal(barrier, inc=1, device_id=dev, device_id_type=MESH)
+    for s in range(1, SUB):
         for copy in fetch(s):
             copy.start()
     fetch_nb.start()
-
-    barrier = pltpu.get_barrier_semaphore()
-    peers = [(pole, nxt), (pole, prv)]
-    peers += [at_xc(d)[1] for d in range(1, 8)]
-    peers += [at_y(d) for d in range(1, 4)]
-    peers += [at_z(d) for d in range(1, 8)]
-    for dev in peers:
-        pl.semaphore_signal(barrier, inc=1, device_id=dev, device_id_type=MESH)
 
     def send(src, dst, s_sem, r_sem, dev):
         return pltpu.make_async_remote_copy(
@@ -273,7 +277,9 @@
     hand.wait_recv()
     term[own, xrows] = term[own, xrows] + from_y[...]
     mine = term[own] + near_l[1] + near_r[1]
-    out_ref[...] = mine
+    held[...] = mine
+    leave = pltpu.make_async_copy(held, out_ref, out_sem)
+    leave.start()
 
     parts = pair(mine)
     four = lax.dot_general(parts, parts, (((0,), (0,)), ((), ())), preferred_element_type=F32)
@@ -286,8 +292,8 @@
     for d in range(1, 8):
         t, dev = at_xc(d)
         copies2.append(send(local.at[rows_of(t)], slot2.at[d - 1], send2.at[d - 1], recv2.at[d - 1], dev))
-    for copy in copies2:
-        copy.start()
+    for d in EIGHT:
+        copies2[d - 1].start()
     total = local[rows_of(here)]
     for d in range(7):
         copies2[d].wait_recv()
@@ -297,8 +303,8 @@
     copies3 = [
         send(acc2, slot3.at[d - 1], send3.at[d - 1], recv3.at[d - 1], at_y(d)) for d in range(1, 4)
     ]
-    for copy in copies3:
-        copy.start()
+    for d in FOUR:
+        copies3[d - 1].start()
     for d in range(3):
         copies3[d].wait_recv()
         total = total + slot3[d]
@@ -307,8 +313,8 @@
     copies4 = [
         send(acc3, slot4.at[d - 1], send4.at[d - 1], recv4.at[d - 1], at_z(d)) for d in range(1, 8)
     ]
-    for copy in copies4:
-        copy.start()
+    for d in EIGHT:
+        copies4[d - 1].start()
     for d in range(7):
         copies4[d].wait_recv()
         total = total + slot4[d]
@@ -319,8 +325,8 @@
         send(part, gram_ref.at[rows_of(here)], send5.at[d - 1], recv5.at[d - 1], at_xc(d)[1])
         for d in range(1, 8)
     ]
-    for copy in copies5:
-        copy.start()
+    for d in EIGHT:
+        copies5[d - 1].start()
     hand.wait_send()
     for kind in range(3):
         for copy in far(kind) + near(kind, 0) + near(kind, 1):
@@ -329,11 +335,9 @@
         cross(shift).wait_send()
     for copy in copies2 + copies3 + copies4:
         copy.wait_send()
+    leave.wait()
     for copy in copies5:
         copy.wait()
-
-
-PIECE = VEC // 8
 
 
 def filter_call(neighbors, pole_weights, iface_rows, couplings, start, inverses):
@@ -349,7 +353,7 @@
             jax.ShapeDtypeStruct((VEC, VEC), F32),
         ),
         in_specs=[hbm, smem, vmem, vmem, hbm, hbm],
-        out_specs=(vmem, vmem),
+        out_specs=(hbm, vmem),
         scratch_shapes=[
             pltpu.SMEM((2, SUB), jnp.int32),
             pltpu.VMEM((SUB, BLK, BLK), F32),
@@ -366,6 +370,7 @@
             pltpu.VMEM((2, BLK, VEC), F32),
             pltpu.VMEM((NX, YROWS, VEC), F32),
             pltpu.VMEM((XROWS, VEC), F32),
+            pltpu.VMEM((BLK, VEC), F32),
             pltpu.VMEM((VEC, VEC), F32),
             pltpu.VMEM((7, PIECE, VEC), F32),
             pltpu.VMEM((3, PIECE, VEC), F32),
@@ -373,7 +378,7 @@
             pltpu.VMEM((PIECE, VEC), F32),
             pltpu.VMEM((PIECE, VEC), F32),
             pltpu.VMEM((PIECE, VEC), F32),
-            dma((SUB,)), dma((SUB,)), dma,
+            dma((SUB,)), dma((SUB,)), dma, dma,
             dma((2, SUB)), dma((2, SUB)),
             dma((2, 3)), dma((2, 3)),
             dma((2, 3, 2)), dma((2, 3, 2)),
@@ -388,52 +393,98 @@
 
 
 TILE = 8
+PANEL = 16
+CLOSE = 2
 
 
 def spread(row):
     return jnp.broadcast_to(row, (TILE, VEC))
 
 
+def three(value):
+    first = value.astype(BF16)
+    rest = value - first.astype(F32)
+    second = rest.astype(BF16)
+    return first, second, (rest - second.astype(F32)).astype(BF16)
+
+
+def six_terms(a, b, axis):
+    a1, a2, a3 = three(a)
+    b1, b2, b3 = three(b)
+    return (
+        jnp.concatenate([a1, a1, a2, a1, a3, a2], axis=axis),
+        jnp.concatenate([b1, b2, b1, b3, b1, b2], axis=axis),
+    )
+
+
 def ortho_kernel(scale, g_ref, f_ref, out_ref, w_ref):
-    count = VEC // TILE
+    count, tall = VEC // TILE, PANEL // TILE
     tiles = [g_ref[TILE * t : TILE * t + TILE, :] for t in range(count)]
     sub = lax.broadcasted_iota(jnp.int32, (TILE, VEC), 0)
     lane = lax.broadcasted_iota(jnp.int32, (TILE, VEC), 1)
-    for p in range(count):
+    below = [(sub > k).astype(F32) for k in range(TILE)]
+    for p in range(0, count, tall):
         c0 = TILE * p
+        own = list(range(p, p + tall))
+        close = list(range(p + tall, min(count, p + tall + CLOSE)))
         cols = {
             (m, t): jnp.broadcast_to(tiles[t][:, c0 + m : c0 + m + 1], (TILE, VEC))
-            for t in range(p, count)
-            for m in range(TILE)
+            for t in own + close
+            for m in range(PANEL)
         }
-        panel = (lane >= c0) & (lane < c0 + TILE)
-        pivots = jnp.ones((TILE, VEC), F32)
-        top = jnp.where(panel, (lane - c0 == sub).astype(F32), tiles[p])
-        factors = {}
-        for k in range(TILE):
-            pivot = spread(cols[k, p][k : k + 1])
-            pivots = jnp.where(sub == k, pivot, pivots)
+        panel = (lane >= c0) & (lane < c0 + PANEL)
+        top = {t: jnp.where(panel, (lane == sub + TILE * t).astype(F32), tiles[t]) for t in own}
+        pivots = {t: jnp.ones((TILE, VEC), F32) for t in own}
+        inverses = dict(pivots)
+        factors, rows = {}, []
+        for k in range(PANEL):
+            t0, r = p + k // TILE, k % TILE
+            pivot = spread(cols[k, t0][r : r + 1])
             inverse = 1.0 / pivot
-            upper = {m: spread(cols[m, p][k : k + 1]) for m in range(k + 1, TILE)}
-            f = jnp.where(sub > k, cols[k, p] * inverse, 0.0)
-            for m in range(k + 1, TILE):
-                cols[m, p] = cols[m, p] - f * upper[m]
-            top = top - f * spread(top[k : k + 1])
-            for t in range(p + 1, count):
+            pivots[t0] = jnp.where(sub == r, pivot, pivots[t0])
+            inverses[t0] = jnp.where(sub == r, inverse, inverses[t0])
+            upper = {m: spread(cols[m, t0][r : r + 1]) for m in range(k + 1, PANEL)}
+            row = spread(top[t0][r : r + 1])
+            rows.append(row)
+            for t in range(t0, p + tall):
+                for m in range(k + 1, PANEL):
+                    cols[m, t] = cols[m, t] - (cols[k, t] * upper[m]) * inverse
+                column = cols[k, t] * below[r] if t == t0 else cols[k, t]
+                top[t] = top[t] - (column * row) * inverse
+            for t in close:
                 f = cols[k, t] * inverse
                 factors[k, t] = f
-                for m in range(k + 1, TILE):
+                for m in range(k + 1, PANEL):
                     cols[m, t] = cols[m, t] - f * upper[m]
-        rows = [spread(top[k : k + 1]) for k in range(TILE)]
-        for t in range(p + 1, count):
-            value = jnp.where(panel, 0.0, tiles[t])
-            for k in range(TILE):
-                value = value - factors[k, t] * rows[k]
-            tiles[t] = value
-        w_ref[c0 : c0 + TILE, :] = jnp.where(lane <= sub + c0, top * (scale * lax.rsqrt(pivots)), 0.0)
-    out_ref[...] = lax.dot_general(
-        f_ref[...], w_ref[...], (((1,), (1,)), ((), ())), precision=precise, preferred_element_type=F32
+        for t in close:
+            terms = [factors[k, t] * rows[k] for k in range(PANEL)]
+            while len(terms) > 1:
+                terms = [terms[i] + terms[i + 1] for i in range(0, len(terms), 2)]
+            tiles[t] = jnp.where(panel, 0.0, tiles[t]) - terms[0]
+        distant = p + tall + CLOSE
+        if distant < count:
+            final = jnp.concatenate([top[t] for t in own], axis=0)
+            a, b = six_terms(final * jnp.concatenate([inverses[t] for t in own], axis=0), final, 0)
+            update = lax.dot_general(a, b, (((0,), (0,)), ((), ())), preferred_element_type=F32)
+            for t in range(distant, count):
+                tiles[t] = jnp.where(panel, 0.0, tiles[t]) - update[TILE * t : TILE * t + TILE]
+        for t in own:
+            w_ref[TILE * t : TILE * t + TILE, :] = jnp.where(
+                lane <= sub + TILE * t, top[t] * (scale * lax.rsqrt(pivots[t])), 0.0
+            )
+    a1, a2, a3 = three(f_ref[...])
+    b1, b2, b3 = three(w_ref[...])
+    along = (((1,), (1,)), ((), ()))
+    wide = lax.dot_general(
+        jnp.concatenate([a1, a2], axis=1),
+        jnp.concatenate([jnp.concatenate([b1, b1], axis=1), jnp.concatenate([b2, b2], axis=1)], axis=0),
+        along, preferred_element_type=F32,
     )
+    small = lax.dot_general(
+        jnp.concatenate([a1, a3], axis=1), jnp.concatenate([b3, b1], axis=1),
+        along, preferred_element_type=F32,
+    )
+    out_ref[...] = wide[:, :VEC] + (wide[:, VEC:] + small)
 
 
 def ortho_call(gram_matrix, filtered, scale):

time: 60.6 us -> 58.2 us (0.960)
  Pallas kernels: 59.7 us -> 57.3 us
    pallas_call x1, Pallas kernels: 6.23 us -> 4.69 us  [ortho_call(): pl.pallas_call(functools.partial(ortho_kernel, scale), name='ortho', out_...]
    pallas_call x1, Pallas kernels: 53.5 us -> 52.6 us  [filter_call(): pl.pallas_call(filter_kernel, name='filter_pass', out_shape=(jax.ShapeDty...]
where the time goes in v4:
time: 58.2 us; the launch traced here: 58 us
  Pallas kernels  57.3 us (98%)
  between operations  0.66 us (1%)
    pallas_call x1, Pallas kernels, filter_call(): pl.pallas_call(filter_kernel, name='filter_pass', out_shape=(jax.ShapeDty...  52.6 us
    pallas_call x1, Pallas kernels, ortho_call(): pl.pallas_call(functools.partial(ortho_kernel, scale), name='ortho', out_...  4.69 us

profile of v4, /device:TPU:1, one launch (start us, length us, event | category | flops | bytes accessed | tf_op | source)
XLA Modules:
  0.0 58.0 jit_solution(15981740717280218445)
XLA Ops:
  0.7 52.6 %filter_pass.1 = (f32[512,128]{1,0:T(8,128)}, f32[128,128]{1,0:T(8,128)}) custom-call(s32[2,8]{1,0:T(2,128)} %bitcast.5, f32[1]{0:T(128)S(6)} %copy.7.w_ref, s32[8,2,128]{2,1,0:T(2,128)} %rows_ref.1, f32[8,2,128]{2,1,0:T(2,128)} %coup_ref.1, f32[8,512,128]{2,1,0:T(8,128)} %bitcast.4, f32[8,512,512]{2,1,0:T(8,128)} %bitcast.3), custom_call_target="tpu_custom_call" | custom-call | tf_op jit(solution)/shard_map/filter_pass/pallas_call | solution.py:348
  53.3 4.7 %ortho.1 = f32[512,128]{1,0:T(8,128)} custom-call(f32[128,128]{1,0:T(8,128)} %get-tuple-element.7.g_ref, f32[512,128]{1,0:T(8,128)} %get-tuple-element.8.f_ref), custom_call_target="tpu_custom_call" | custom-call | tf_op jit(solution)/shard_map/ortho/pallas_call | solution.py:492

commit v5 on v4

--- a/solution.py
+++ b/solution.py
@@ -45,10 +45,10 @@
 
 
 def filter_kernel(
-    nb_hbm, w_ref, rows_ref, coup_ref, start_ref, inv_ref, out_ref, gram_ref,
-    nb_ref, a32, ahl, b32, outgoing, arrived, term, far_l, far_r, far_l2, far_r2, near_l, near_r, crossed, from_y, held,
+    nb_hbm, w_hbm, rows_hbm, coup_hbm, start_ref, inv_ref, out_ref, gram_ref,
+    nb_ref, w_ref, rows_ref, coup_ref, a32, ahl, b32, outgoing, arrived, term, far_l, far_r, far_l2, far_r2, near_l, near_r, crossed, from_y, held,
     local, slot2, slot3, slot4, acc2, acc3, part,
-    a_sem, b_sem, nb_sem, out_sem, ex_send, ex_recv, far_send, far_recv, near_send, near_recv,
+    round_sem, a_sem, b_sem, small_sem, out_sem, ex_send, ex_recv, far_send, far_recv, near_send, near_recv,
     cross_send, cross_recv, y_send, y_recv, send2, recv2, send3, recv3, send4, recv4, send5, recv5,
 ):
     pole = lax.axis_index("pole")
@@ -85,20 +85,31 @@
             pltpu.make_async_copy(start_ref.at[s], b32.at[s], b_sem.at[s]),
         )
 
-    fetch_nb = pltpu.make_async_copy(nb_hbm, nb_ref, nb_sem)
+    small = [
+        pltpu.make_async_copy(src, dst, small_sem.at[i])
+        for i, (src, dst) in enumerate(
+            ((rows_hbm, rows_ref), (coup_hbm, coup_ref), (nb_hbm, nb_ref), (w_hbm, w_ref))
+        )
+    ]
     for copy in fetch(0):
         copy.start()
+    for copy in small:
+        copy.start()
     barrier = pltpu.get_barrier_semaphore()
-    peers = [at_z(d) for d in EIGHT]
-    peers += [(pole, nxt), (pole, prv)]
-    peers += [at_y(d) for d in FOUR]
-    peers += [at_xc(d)[1] for d in EIGHT]
+    z_near = (at_z(1), at_z(7))
+    peers = [(pole, nxt), (pole, prv), *z_near, at_y(1), at_y(3), (right, sub), (left, sub)]
     for dev in peers:
         pl.semaphore_signal(barrier, inc=1, device_id=dev, device_id_type=MESH)
     for s in range(1, SUB):
         for copy in fetch(s):
             copy.start()
-    fetch_nb.start()
+
+    def tell(n):
+        for dev in z_near:
+            pl.semaphore_signal(round_sem.at[n], inc=1, device_id=dev, device_id_type=MESH)
+
+    def hear(n):
+        pl.semaphore_wait(round_sem.at[n], 2)
 
     def send(src, dst, s_sem, r_sem, dev):
         return pltpu.make_async_remote_copy(
@@ -137,13 +148,17 @@
         @pl.when(s == 0)
         def _():
             pl.semaphore_wait(barrier, len(peers))
+            tell(0)
 
         for side in range(2):
             exchange(side, s).start()
         return carry
 
+    for copy in small:
+        copy.wait()
     lax.fori_loop(0, SUB, first, 0)
-    fetch_nb.wait()
+    hear(0)
+    tell(1)
 
     def arrive(s, carry):
         exchange(0, s).wait()
@@ -253,6 +268,8 @@
         return carry
 
     lax.fori_loop(0, SUB, sequence, 0)
+    hear(1)
+    tell(2)
 
     join(2)
     for copy in far(2) + near(1, 0):
@@ -280,6 +297,7 @@
     held[...] = mine
     leave = pltpu.make_async_copy(held, out_ref, out_sem)
     leave.start()
+    hear(2)
 
     parts = pair(mine)
     four = lax.dot_general(parts, parts, (((0,), (0,)), ((), ())), preferred_element_type=F32)
@@ -343,8 +361,7 @@
 def filter_call(neighbors, pole_weights, iface_rows, couplings, start, inverses):
     dma = pltpu.SemaphoreType.DMA
     vmem = pl.BlockSpec(memory_space=pltpu.VMEM)
-    smem = pl.BlockSpec(memory_space=pltpu.SMEM)
-    hbm = pl.BlockSpec(memory_space=pl.ANY)
+    hbm = pl.BlockSpec(memory_space=pltpu.HBM)
     return pl.pallas_call(
         filter_kernel,
         name="filter_pass",
@@ -352,10 +369,13 @@
             jax.ShapeDtypeStruct((BLK, VEC), F32),
             jax.ShapeDtypeStruct((VEC, VEC), F32),
         ),
-        in_specs=[hbm, smem, vmem, vmem, hbm, hbm],
+        in_specs=[hbm] * 6,
         out_specs=(hbm, vmem),
         scratch_shapes=[
             pltpu.SMEM((2, SUB), jnp.int32),
+            pltpu.SMEM((1,), F32),
+            pltpu.VMEM((SUB, 2, IFC), jnp.int32),
+            pltpu.VMEM((SUB, 2, IFC), F32),
             pltpu.VMEM((SUB, BLK, BLK), F32),
             pltpu.VMEM((SUB, BLK, 2 * BLK), BF16),
             pltpu.VMEM((SUB, BLK, VEC), F32),
@@ -378,7 +398,8 @@
             pltpu.VMEM((PIECE, VEC), F32),
             pltpu.VMEM((PIECE, VEC), F32),
             pltpu.VMEM((PIECE, VEC), F32),
-            dma((SUB,)), dma((SUB,)), dma, dma,
+            pltpu.SemaphoreType.REGULAR((3,)),
+            dma((SUB,)), dma((SUB,)), dma((4,)), dma,
             dma((2, SUB)), dma((2, SUB)),
             dma((2, 3)), dma((2, 3)),
             dma((2, 3, 2)), dma((2, 3, 2)),

time: 58.2 us -> 57.2 us (0.983)
  Pallas kernels: 57.3 us -> 56.4 us
    pallas_call x1, Pallas kernels: 52.6 us -> 51.7 us  [filter_call(): pl.pallas_call(filter_kernel, name='filter_pass', out_shape=(jax.ShapeDty...]
where the time goes in v5:
time: 57.2 us; the launch traced here: 57 us
  Pallas kernels  56.4 us (99%)
  between operations  0.66 us (1%)
    pallas_call x1, Pallas kernels, filter_call(): pl.pallas_call(filter_kernel, name='filter_pass', out_shape=(jax.ShapeDty...  51.7 us
    pallas_call x1, Pallas kernels, ortho_call(): pl.pallas_call(functools.partial(ortho_kernel, scale), name='ortho', out_...  4.69 us

profile of v5, /device:TPU:1, one launch (start us, length us, event | category | flops | bytes accessed | tf_op | source)
XLA Modules:
  0.0 57.0 jit_solution(339849385206755849)
XLA Ops:
  0.7 51.7 %filter_pass.1 = (f32[512,128]{1,0:T(8,128)}, f32[128,128]{1,0:T(8,128)}) custom-call(s32[2,8]{1,0:T(2,128)} %bitcast.5, f32[1]{0:T(128)S(6)} %copy.7.w_hbm, s32[8,2,128]{2,1,0:T(2,128)} %rows_hbm.1, f32[8,2,128]{2,1,0:T(2,128)} %coup_hbm.1, f32[8,512,128]{2,1,0:T(8,128)} %bitcast.4, f32[8,512,512]{2,1,0:T(8,128)} %bitcast.3), custom_call_target="tpu_custom_call" | custom-call | tf_op jit(solution)/shard_map/filter_pass/pallas_call | solution.py:365
  52.3 4.7 %ortho.1 = f32[512,128]{1,0:T(8,128)} custom-call(f32[128,128]{1,0:T(8,128)} %get-tuple-element.7.g_ref, f32[512,128]{1,0:T(8,128)} %get-tuple-element.8.f_ref), custom_call_target="tpu_custom_call" | custom-call | tf_op jit(solution)/shard_map/ortho/pallas_call | solution.py:513

commit v6 on v5

--- a/solution.py
+++ b/solution.py
@@ -48,7 +48,7 @@
     nb_hbm, w_hbm, rows_hbm, coup_hbm, start_ref, inv_ref, out_ref, gram_ref,
     nb_ref, w_ref, rows_ref, coup_ref, a32, ahl, b32, outgoing, arrived, term, far_l, far_r, far_l2, far_r2, near_l, near_r, crossed, from_y, held,
     local, slot2, slot3, slot4, acc2, acc3, part,
-    round_sem, a_sem, b_sem, small_sem, out_sem, ex_send, ex_recv, far_send, far_recv, near_send, near_recv,
+    round_sem, a_sem, b_sem, small_sem, out_sem, keep_sem, ex_send, ex_recv, far_send, far_recv, near_send, near_recv,
     cross_send, cross_recv, y_send, y_recv, send2, recv2, send3, recv3, send4, recv4, send5, recv5,
 ):
     pole = lax.axis_index("pole")
@@ -337,7 +337,8 @@
         copies4[d].wait_recv()
         total = total + slot4[d]
     part[...] = total
-    gram_ref[rows_of(here)] = total
+    keep = pltpu.make_async_copy(part, gram_ref.at[rows_of(here)], keep_sem)
+    keep.start()
 
     copies5 = [
         send(part, gram_ref.at[rows_of(here)], send5.at[d - 1], recv5.at[d - 1], at_xc(d)[1])
@@ -354,13 +355,13 @@
     for copy in copies2 + copies3 + copies4:
         copy.wait_send()
     leave.wait()
+    keep.wait()
     for copy in copies5:
         copy.wait()
 
 
 def filter_call(neighbors, pole_weights, iface_rows, couplings, start, inverses):
     dma = pltpu.SemaphoreType.DMA
-    vmem = pl.BlockSpec(memory_space=pltpu.VMEM)
     hbm = pl.BlockSpec(memory_space=pltpu.HBM)
     return pl.pallas_call(
         filter_kernel,
@@ -370,7 +371,7 @@
             jax.ShapeDtypeStruct((VEC, VEC), F32),
         ),
         in_specs=[hbm] * 6,
-        out_specs=(hbm, vmem),
+        out_specs=(hbm, hbm),
         scratch_shapes=[
             pltpu.SMEM((2, SUB), jnp.int32),
             pltpu.SMEM((1,), F32),
@@ -399,7 +400,7 @@
             pltpu.VMEM((PIECE, VEC), F32),
             pltpu.VMEM((PIECE, VEC), F32),
             pltpu.SemaphoreType.REGULAR((3,)),
-            dma((SUB,)), dma((SUB,)), dma((4,)), dma,
+            dma((SUB,)), dma((SUB,)), dma((4,)), dma, dma,
             dma((2, SUB)), dma((2, SUB)),
             dma((2, 3)), dma((2, 3)),
             dma((2, 3, 2)), dma((2, 3, 2)),

time: 57.2 us -> 56.7 us (level)
  no operation moved by 1% of the time
where the time goes in v6:
time: 56.7 us; the launch traced here: 56.5 us
  Pallas kernels  55.9 us (99%)
  between operations  0.66 us (1%)
    pallas_call x1, Pallas kernels, filter_call(): pl.pallas_call(filter_kernel, name='filter_pass', out_shape=(jax.ShapeDty...  51.2 us
    pallas_call x1, Pallas kernels, ortho_call(): pl.pallas_call(functools.partial(ortho_kernel, scale), name='ortho', out_...  4.69 us

profile of v6, /device:TPU:1, one launch (start us, length us, event | category | flops | bytes accessed | tf_op | source)
XLA Modules:
  0.0 56.5 jit_solution(7308032858904815942)
XLA Ops:
  0.7 51.2 %filter_pass.1 = (f32[512,128]{1,0:T(8,128)}, f32[128,128]{1,0:T(8,128)}) custom-call(s32[2,8]{1,0:T(2,128)} %bitcast.5, f32[1]{0:T(128)S(6)} %copy.7.w_hbm, s32[8,2,128]{2,1,0:T(2,128)} %rows_hbm.1, f32[8,2,128]{2,1,0:T(2,128)} %coup_hbm.1, f32[8,512,128]{2,1,0:T(8,128)} %bitcast.4, f32[8,512,512]{2,1,0:T(8,128)} %bitcast.3), custom_call_target="tpu_custom_call" | custom-call | tf_op jit(solution)/shard_map/filter_pass/pallas_call | solution.py:366
  51.8 4.7 %ortho.1 = f32[512,128]{1,0:T(8,128)} custom-call(f32[128,128]{1,0:T(8,128)} %get-tuple-element.7.g_ref, f32[512,128]{1,0:T(8,128)} %get-tuple-element.8.f_ref), custom_call_target="tpu_custom_call" | custom-call | tf_op jit(solution)/shard_map/ortho/pallas_call | solution.py:514

commit v7 on v6

--- a/solution.py
+++ b/solution.py
@@ -235,7 +235,7 @@
         shift = jnp.where((i == 4) | (i == 7), 0, shift)
         kind = jnp.where((i == 1) | (i > 4), 1, 0)
 
-        @pl.when(i == 7)
+        @pl.when(i == 6)
         def _():
             relay(0)
 

time: 56.7 us -> 56.5 us (level)
  no operation moved by 1% of the time
where the time goes in v7:
time: 56.5 us; the launch traced here: 56.3 us
  Pallas kernels  55.7 us (99%)
  between operations  0.66 us (1%)
    pallas_call x1, Pallas kernels, filter_call(): pl.pallas_call(filter_kernel, name='filter_pass', out_shape=(jax.ShapeDty...  51 us
    pallas_call x1, Pallas kernels, ortho_call(): pl.pallas_call(functools.partial(ortho_kernel, scale), name='ortho', out_...  4.69 us

profile of v7, /device:TPU:1, one launch (start us, length us, event | category | flops | bytes accessed | tf_op | source)
XLA Modules:
  0.0 56.3 jit_solution(9208016640031555674)
XLA Ops:
  0.7 51.0 %filter_pass.1 = (f32[512,128]{1,0:T(8,128)}, f32[128,128]{1,0:T(8,128)}) custom-call(s32[2,8]{1,0:T(2,128)} %bitcast.5, f32[1]{0:T(128)S(6)} %copy.7.w_hbm, s32[8,2,128]{2,1,0:T(2,128)} %rows_hbm.1, f32[8,2,128]{2,1,0:T(2,128)} %coup_hbm.1, f32[8,512,128]{2,1,0:T(8,128)} %bitcast.4, f32[8,512,512]{2,1,0:T(8,128)} %bitcast.3), custom_call_target="tpu_custom_call" | custom-call | tf_op jit(solution)/shard_map/filter_pass/pallas_call | solution.py:366
  51.6 4.7 %ortho.1 = f32[512,128]{1,0:T(8,128)} custom-call(f32[128,128]{1,0:T(8,128)} %get-tuple-element.7.g_ref, f32[512,128]{1,0:T(8,128)} %get-tuple-element.8.f_ref), custom_call_target="tpu_custom_call" | custom-call | tf_op jit(solution)/shard_map/ortho/pallas_call | solution.py:514
